TPU v7x, 128 devices: a whole 4x4x4 slice. The times are simulated.
128 devices in a mesh: pipe: 2 (over x_lo), dp: 64 (over z, x_hi, y, core).
Axes of the slice: x: 4 (x_hi: 2, x_lo: 2; x = x_hi * 2 + x_lo), y: 4, z: 4, core: 2. Of those that a mesh axis runs over, the one named last changes fastest.
Arguments:
- segment_input: bfloat16 [2, 512, 12288], P('pipe', 'dp'), may hold values from -3000 to 3000, as said below
- norm_gain: float32 [2, 12288], P('pipe'), may hold values from 0.5 to 2
- head_weights: bfloat16 [2, 12288, 64, 384], P('pipe', None, 'dp'), may hold values from -0.04818163 to 0.04818163
- output_weights: bfloat16 [2, 8192, 12288], P('pipe', 'dp'), may hold values from -0.25 to 0.25
Outputs:
- section_outputs: bfloat16 [2, 512, 12288], P('pipe', 'dp')
Inputs may be any that keep to these rules, and one draw needn't show every extreme that they name: `segment_input`: activations of order one to some thousands, rows and features of unlike scales.
All inputs are finite; a program needn't handle non-finite values.
Results may differ from a plain program's by a relative error of at most 0.0083.
Values may be sent and summed in bfloat16 or wider, within the bound.
No kernel may reach another device: no remote copies, remote signals or barrier semaphores. Data moves between devices by JAX's collectives and lax.ppermute only.
A program may use at most 128 MiB of HBM per device.

v0:
```python
import math
import jax
import jax.numpy as jnp
from jax import lax
from jax.sharding import PartitionSpec as P


def from_behind(value, axis, steps):
    count = lax.axis_size(axis)
    pairs = [(source, (source + steps) % count) for source in range(count)]
    return lax.ppermute(value, axis, pairs)


def normalize(section_rows, gain_vector):
    values = section_rows.astype(jnp.float32)
    centre = jnp.mean(values, axis=-1, keepdims=True)
    shifted = values - centre
    spread = jnp.mean(shifted * shifted, axis=-1, keepdims=True)
    return (shifted * lax.rsqrt(spread + 1e-05) * gain_vector).astype(jnp.bfloat16)


def attend(projected, head_size):
    queries = projected[:, :head_size]
    keys_part = projected[:, head_size : 2 * head_size]
    values_part = projected[:, 2 * head_size :].astype(jnp.bfloat16)
    scores = jnp.einsum(
        "qd,kd->qk", queries, keys_part, precision=lax.Precision.HIGHEST
    ) / math.sqrt(head_size)
    length = projected.shape[0]
    causal = jnp.arange(length)[:, None] >= jnp.arange(length)[None, :]
    scores = jnp.where(causal, scores, -1e30)
    largest = jnp.max(scores, axis=-1, keepdims=True)
    weights = jnp.where(causal, jnp.exp(scores - largest), 0.0)
    totals = jnp.sum(weights, axis=-1, keepdims=True)
    probabilities = (weights / totals).astype(jnp.bfloat16)
    return jnp.dot(probabilities, values_part, preferred_element_type=jnp.float32).astype(
        jnp.bfloat16
    )


def shards(segment_input, norm_gain, head_weights, output_weights):
    head_size = output_weights.shape[1]
    normed = normalize(segment_input[0], norm_gain[0])
    head_block = head_weights[0, :, 0, :]
    projected = jnp.dot(
        lax.all_gather(normed, "dp", axis=0, tiled=True),
        head_block,
        preferred_element_type=jnp.float32,
    )
    attended = attend(projected, head_size)
    out_rows = output_weights[0]
    finished = lax.psum_scatter(
        jnp.dot(attended, out_rows, preferred_element_type=jnp.float32),
        "dp",
        scatter_dimension=0,
        tiled=True,
    ).astype(jnp.bfloat16)
    handed = from_behind(finished, "pipe", 1)
    return handed[None]


def solution(mesh):
    placed = (
        P("pipe", "dp", None),
        P("pipe", None),
        P("pipe", None, "dp", None),
        P("pipe", "dp", None),
    )
    return jax.shard_map(
        shards, mesh=mesh, in_specs=placed, out_specs=P("pipe", "dp", None), check_vma=False
    )
```

profile of v0, /device:TPU:0, one launch (start us, length us, event | category | flops | bytes accessed | tf_op | source)
XLA Modules:
  0.0 382.8 jit_solution(5650053508658786681)
XLA Ops:
  6.5 0.0 copy-start
  6.5 0.0 all-gather.2.cloned.1.call-start
  6.5 1.3 convert_reduce_fusion
  7.8 1.2 fusion.15
  9.1 1.7 fusion.17
  10.8 0.0 all-gather.2.cloned.1.call-update
  10.8 0.0 reduce-scatter.2.cloned.1.call-start
  10.9 95.6 %all-gather.2.cloned.1.call-done = bf16[512,12288]{1,0:T(8,128)(2,1)} async-done(((bf16[8,12288]{1,0:T(8,128)(2,1)}), bf16[512,12288]{1,0:T(8,128)(2,1)}) %all-gather.2.cloned.1.call-update) | async-done | bytes 12582928 | tf_op jit(solution)/shard_map/all_gather | solution.py:46
  106.5 12.7 %fusion = f32[512,384]{1,0:T(8,128)S(1)} fusion(bf16[512,12288]{1,0:T(8,128)(2,1)} %all-gather.2.cloned.1.call-done, bf16[1,12288,1,384]{3,1,2,0:T(8,128)(2,1)} %param.6), kind=kOutput, calls=%fused_computation | convolution fusion | flops 4831838208 | bytes 22806528 | tf_op jit(solution)/shard_map/dot_general | solution.py:45
  119.2 0.0 copy-start.2
  119.2 0.9 copy-done.2
  120.1 1.0 fusion.22
  121.1 0.0 copy-start.1
  121.1 1.1 copy-done.1
  122.2 0.2 fusion.5
  122.3 0.0 copy-done
  122.3 11.8 %fusion.2 = f32[512,12288]{1,0:T(8,128)} fusion(bf16[1,128,12288]{2,1,0:T(8,128)(2,1)S(1)} %copy-done, f32[512,512]{0,1:T(8,128)} %copy-done.1, f32[512]{0:T(512)S(1)} %fusion.5, f32[512]{0:T(512)S(1)} %get-tuple-element.5, f32[512,384]{1,0:T(8,128)} %copy-done.2), kind=kOutput, calls=%fused_computation.2 | convolution fusion | flops 1679097856 | bytes 29495296 | tf_op jit(solution)/shard_map/dot_general | solution.py:53
  134.1 0.0 reduce-scatter.2.cloned.1.call-update
  134.1 234.4 %reduce-scatter.2.cloned.1.call-done = f32[8,12288]{1,0:T(8,128)} async-done(((f32[512,12288]{1,0:T(8,128)}), f32[8,12288]{1,0:T(8,128)}) %reduce-scatter.2.cloned.1.call-update) | async-done | bytes 393232 | tf_op jit(solution)/shard_map/reduce_scatter | solution.py:52
  368.5 1.0 convert_element_type.24
  369.6 0.6 collective-permute-start
  370.2 5.1 %collective-permute-done = bf16[8,12288]{1,0:T(8,128)(2,1)S(1)} collective-permute-done((bf16[8,12288]{1,0:T(8,128)(2,1)S(1)}, bf16[8,12288]{1,0:T(8,128)(2,1)S(1)}, u32[]{:S(2)}, u32[]{:S(2)}) %collective-permute-start) | collective-permute-done | bytes 196640 | tf_op jit(solution)/shard_map/ppermute | solution.py:11
  375.3 0.7 copy.6
  (2 shorter events, 0.0 us)
Async XLA Ops:
  6.5 115.8 %copy-start = (bf16[1,128,12288]{2,1,0:T(8,128)(2,1)S(1)}, bf16[1,128,12288]{2,1,0:T(8,128)(2,1)}, u32[]{:S(2)}) copy-start(bf16[1,128,12288]{2,1,0:T(8,128)(2,1)} %param.7) | copy-start | bytes 9437188
  6.5 100.0 %all-gather.2.cloned.1.call-start = ((), (), s32[]{:S(2)}) async-start(), calls=%async_computation.1 | async-start | bytes 12779520 | tf_op jit(solution)/shard_map/all_gather | solution.py:46
  10.8 357.7 %reduce-scatter.2.cloned.1.call-start = ((), (), s32[]{:S(2)}) async-start(), calls=%async_computation.2 | async-start | bytes 25559040 | tf_op jit(solution)/shard_map/reduce_scatter | solution.py:52
  119.2 0.9 copy-start.2
  121.1 1.1 copy-start.1
  369.6 5.7 %collective-permute-start = (bf16[8,12288]{1,0:T(8,128)(2,1)S(1)}, bf16[8,12288]{1,0:T(8,128)(2,1)S(1)}, u32[]{:S(2)}, u32[]{:S(2)}) collective-permute-start(bf16[8,12288]{1,0:T(8,128)(2,1)S(1)} %convert_element_type.24), channel_id=1, source_target_pairs={{0,64},{64,0},{1,65},{65,1},{2,66},{66,2},{3,67},{67,3},{4,68},{68... | collective-permute-start | bytes 589832 | tf_op jit(solution)/shard_map/ppermute | solution.py:11
Sparse Core Ops, SparseCore 0:
  10.9 95.5 all-gather.1
  134.2 234.2 reduce-scatter.1
where the time goes:
time: 383 us
  waiting for transfers between devices  335 us (87%)
  matrix products  25.5 us (7%)
  between operations  13.4 us (3%)
  other arithmetic  5.42 us (1%)
    reduce_scatter x1, waiting for transfers between devices, shards(): lax.psum_scatter(jnp.dot(attended, out_rows, preferred_element_type=jnp.f...  234 us
    all_gather x1, waiting for transfers between devices, shards(): lax.all_gather(normed, 'dp', axis=0, tiled=True)  95.6 us
    dot_general x1, matrix products, shards(): jnp.dot(lax.all_gather(normed, 'dp', axis=0, tiled=True), head_block, pre...  12.7 us
    dot_general x1, matrix products, shards(): jnp.dot(attended, out_rows, preferred_element_type=jnp.float32)  11.8 us
  transfers between devices with their start and end apart: 3, of which 3 were waited for; matrix products, arithmetic and copies ran while one was open for 0% of the time, Pallas kernels for 0%

commit v1 on v0

--- a/solution.py
+++ b/solution.py
@@ -3,6 +3,13 @@
 import jax.numpy as jnp
 from jax import lax
 from jax.sharding import PartitionSpec as P
+
+
+def move_the_goods(array_dim, matrix):
+    sheets = []
+    for _ in range(lax.psum(1, "dp")):
+        sheets.append(matrix)
+    return jnp.concatenate(lax.all_to_all(jnp.stack(sheets, axis=0), "dp", 0, 0), array_dim)
 
 
 def from_behind(value, axis, steps):
@@ -42,11 +49,7 @@
     head_size = output_weights.shape[1]
     normed = normalize(segment_input[0], norm_gain[0])
     head_block = head_weights[0, :, 0, :]
-    projected = jnp.dot(
-        lax.all_gather(normed, "dp", axis=0, tiled=True),
-        head_block,
-        preferred_element_type=jnp.float32,
-    )
+    projected = jnp.dot(move_the_goods(0, normed), head_block, preferred_element_type=jnp.float32)
     attended = attend(projected, head_size)
     out_rows = output_weights[0]
     finished = lax.psum_scatter(

time: 383 us -> 442 us (1.15)
  blocking collectives: 0 us -> 154 us
  waiting for transfers between devices: 335 us -> 239 us
  local copies, waits for them, and re-layouts: 2.63 us -> 8.71 us
    all_to_all x0 -> x1, blocking collectives: none -> 154 us  [move_the_goods(): lax.all_to_all(jnp.stack(sheets, axis=0), 'dp', 0, 0)]
    all_gather x1 -> x0, waiting for transfers between devices: 95.6 us -> none  [shards(): lax.all_gather(normed, 'dp', axis=0, tiled=True)]
    another operation x0 -> x1, local copies, waits for them, and re-layouts: none -> 6.09 us  [move_the_goods(): jnp.stack(sheets, axis=0)]
  transfers between devices with their start and end apart: 3 -> 2, of which waited for: 3 -> 2; matrix products, arithmetic and copies ran while one was open for 0% -> 0% of each run, Pallas kernels for 0% -> 0%
where the time goes in v1:
time: 442 us
  waiting for transfers between devices  239 us (54%)
  blocking collectives  154 us (35%)
  matrix products  22 us (5%)
  between operations  13.4 us (3%)
  local copies, waits for them, and re-layouts  8.71 us (2%)
  other arithmetic  4.74 us (1%)
    reduce_scatter x1, waiting for transfers between devices, shards(): lax.psum_scatter(jnp.dot(attended, out_rows, preferred_element_type=jnp.f...  233 us
    all_to_all x1, blocking collectives, move_the_goods(): lax.all_to_all(jnp.stack(sheets, axis=0), 'dp', 0, 0)  154 us
    dot_general x1, matrix products, shards(): jnp.dot(attended, out_rows, preferred_element_type=jnp.float32)  11.8 us
    dot_general x1, matrix products, shards(): jnp.dot(move_the_goods(0, normed), head_block, preferred_element_type=jnp...  9.23 us
  transfers between devices with their start and end apart: 2, of which 2 were waited for; matrix products, arithmetic and copies ran while one was open for 0% of the time, Pallas kernels for 0%

profile of v1, /device:TPU:0, one launch (start us, length us, event | category | flops | bytes accessed | tf_op | source)
XLA Modules:
  0.0 442.2 jit_solution(18158575977709054743)
XLA Ops:
  6.5 0.0 copy-start
  6.5 0.0 reduce-scatter.2.cloned.1.call-start
  6.5 1.3 convert_reduce_fusion
  7.8 1.2 fusion.18
  9.1 1.1 fusion.21
  10.1 6.1 %stack.5 = bf16[64,8,12288]{2,1,0:T(8,128)(2,1)} broadcast(bf16[8,12288]{1,0:T(8,128)(2,1)S(1)} %fusion.21), dimensions={1,2} | broadcast | bytes 12779520 | tf_op jit(solution)/shard_map/stack | solution.py:12
  16.2 154.0 %all_to_all.5 = bf16[64,8,12288]{2,1,0:T(8,128)(2,1)S(1)} all-to-all(bf16[64,8,12288]{2,1,0:T(8,128)(2,1)} %stack.5), channel_id=1, replica_groups=mesh['pipe'=2,'dp'=64] {'dp'}, dimensions={0} | all-to-all | bytes 25165824 | tf_op jit(solution)/shard_map/all_to_all | solution.py:12
  170.3 9.2 %fusion = f32[512,384]{1,0:T(8,128)S(1)} fusion(bf16[64,8,12288]{2,1,0:T(8,128)(2,1)S(1)} %all_to_all.5, bf16[1,12288,1,384]{3,1,2,0:T(8,128)(2,1)} %param.6), kind=kOutput, calls=%fused_computation | convolution fusion | flops 4831838208 | bytes 22806528 | tf_op jit(solution)/shard_map/dot_general | solution.py:52
  179.5 0.0 copy-start.2
  179.5 0.9 copy-done.2
  180.4 1.0 fusion.24
  181.4 0.0 copy-start.1
  181.4 1.1 copy-done.1
  182.5 0.2 fusion.6
  182.6 0.0 copy-done
  182.6 11.8 %fusion.3 = f32[512,12288]{1,0:T(8,128)} fusion(bf16[1,128,12288]{2,1,0:T(8,128)(2,1)S(1)} %copy-done, f32[512,512]{0,1:T(8,128)} %copy-done.1, f32[512]{0:T(512)S(1)} %fusion.6, f32[512]{0:T(512)S(1)} %get-tuple-element.5, f32[512,384]{1,0:T(8,128)} %copy-done.2), kind=kOutput, calls=%fused_computation.3 | convolution fusion | flops 1679097856 | bytes 29495296 | tf_op jit(solution)/shard_map/dot_general | solution.py:56
  194.4 0.0 reduce-scatter.2.cloned.1.call-update
  194.4 233.5 %reduce-scatter.2.cloned.1.call-done = f32[8,12288]{1,0:T(8,128)} async-done(((f32[512,12288]{1,0:T(8,128)}), f32[8,12288]{1,0:T(8,128)}) %reduce-scatter.2.cloned.1.call-update) | async-done | bytes 393232 | tf_op jit(solution)/shard_map/reduce_scatter | solution.py:55
  427.9 1.0 convert_element_type.26
  428.9 0.7 collective-permute-start
  429.5 5.1 %collective-permute-done = bf16[8,12288]{1,0:T(8,128)(2,1)S(1)} collective-permute-done((bf16[8,12288]{1,0:T(8,128)(2,1)S(1)}, bf16[8,12288]{1,0:T(8,128)(2,1)S(1)}, u32[]{:S(2)}, u32[]{:S(2)}) %collective-permute-start) | collective-permute-done | bytes 196640 | tf_op jit(solution)/shard_map/ppermute | solution.py:18
  434.6 0.7 copy.6
  (2 shorter events, 0.0 us)
Async XLA Ops:
  6.5 176.1 %copy-start = (bf16[1,128,12288]{2,1,0:T(8,128)(2,1)S(1)}, bf16[1,128,12288]{2,1,0:T(8,128)(2,1)}, u32[]{:S(2)}) copy-start(bf16[1,128,12288]{2,1,0:T(8,128)(2,1)} %param.7) | copy-start | bytes 9437188
  6.5 421.3 %reduce-scatter.2.cloned.1.call-start = ((), (), s32[]{:S(2)}) async-start(), calls=%async_computation.2 | async-start | bytes 25559040 | tf_op jit(solution)/shard_map/reduce_scatter | solution.py:55
  179.5 0.9 copy-start.2
  181.4 1.1 copy-start.1
  428.9 5.7 %collective-permute-start = (bf16[8,12288]{1,0:T(8,128)(2,1)S(1)}, bf16[8,12288]{1,0:T(8,128)(2,1)S(1)}, u32[]{:S(2)}, u32[]{:S(2)}) collective-permute-start(bf16[8,12288]{1,0:T(8,128)(2,1)S(1)} %convert_element_type.26), channel_id=1, source_target_pairs={{0,64},{64,0},{1,65},{65,1},{2,66},{66,2},{3,67},{67,3},{4,68},{68... | collective-permute-start | bytes 589832 | tf_op jit(solution)/shard_map/ppermute | solution.py:18
Sparse Core Ops, SparseCore 0:
  194.5 233.2 reduce-scatter.1
